TPU v7x, 32 devices: a whole 2x2x4 slice. The times are simulated.
32 devices in a mesh: seq: 8 (over y, x, core), mp: 4 (over z).
Axes of the slice: x: 2, y: 2, z: 4, core: 2. Of those that a mesh axis runs over, the one named last changes fastest.
Arguments:
- tokens: bfloat16 [1024, 4096], P('seq', 'mp'), may hold values from -10 to 10
- norm_gain: float32 [4096], replicated, may hold values from 0.1 to 1.9
- w_cand: bfloat16 [4096, 4096], P('seq', 'mp'), may hold values from -0.125 to 0.125
- w_gate: bfloat16 [4096, 4096], P('seq', 'mp'), may hold values from -0.046875 to 0.046875
- rec_gate: float32 [4096], P('mp'), may hold values from -0.75 to 0.75
- rec_cand: float32 [4096], P('mp'), may hold values from -0.6 to 0.6
- bias_gate: float32 [4096], P('mp')
- w_out: bfloat16 [4096, 4096], P('mp'), may hold values from -0.09375 to 0.09375
Outputs:
- output: bfloat16 [1024, 4096], P('seq', 'mp')
All inputs are finite; a program needn't handle non-finite values.
Results may differ from a plain program's by a relative error of at most 0.0048.
Values may be sent and summed in bfloat16 or wider, within the bound.
A program may use at most 64 MiB of HBM per device.

v0:
```python
import jax
import jax.numpy as jnp
from jax import lax
from jax.sharding import PartitionSpec as P

NEWTON = 3


def prefix(value, axis, join, neutral):
    count, mine = (lax.axis_size(axis), lax.axis_index(axis))
    pieces = jax.tree.map(lambda part: lax.all_gather(part, axis), value)
    subtotal = jax.tree.map(
        lambda part, zero: jnp.full_like(part, 0) + jnp.asarray(zero, part.dtype), value, neutral
    )

    def lap(position, subtotal):
        longer = join(subtotal, jax.tree.map(lambda part: part[position], pieces))
        return jax.tree.map(lambda new, old: jnp.where(position < mine, new, old), longer, subtotal)

    return lax.fori_loop(0, count - 1, lap, subtotal)


def compose(earlier, later):
    return (later[0] * earlier[0], later[0] * earlier[1] + later[1])


def cell(previous, cand_pre, gate_pre, rec_gate, rec_cand, bias_gate):
    gate = jax.nn.sigmoid(gate_pre + rec_gate * previous + bias_gate)
    cand = jnp.tanh(cand_pre + rec_cand * previous)
    value = gate * previous + (1.0 - gate) * cand
    slope = (
        gate
        + gate * (1.0 - gate) * rec_gate * (previous - cand)
        + (1.0 - gate) * (1.0 - cand * cand) * rec_cand
    )
    return (value, slope)


def per_device(tokens, norm_gain, w_cand, w_gate, rec_gate, rec_cand, bias_gate, w_out):
    tok_rows = tokens.shape[0]
    channels = w_cand.shape[1]
    whole = lax.all_gather(tokens, "mp", axis=1, tiled=True)
    wide = whole.astype(jnp.float32)
    factor = lax.rsqrt(jnp.mean(wide * wide, axis=1, keepdims=True) + 1e-05)
    normed = (wide * factor * norm_gain).astype(jnp.bfloat16)
    cand_pre = jnp.dot(
        normed,
        lax.all_gather(w_cand, "seq", axis=0, tiled=True),
        preferred_element_type=jnp.float32,
    )
    gate_pre = jnp.dot(
        normed,
        lax.all_gather(w_gate, "seq", axis=0, tiled=True),
        preferred_element_type=jnp.float32,
    )
    state = jnp.zeros((tok_rows, channels), jnp.float32)
    carried = jnp.zeros((channels,), jnp.float32)
    ones_row = jnp.ones((channels,), jnp.float32)
    for newton_step in range(NEWTON):
        previous = jnp.concatenate([carried[None, :], state[:-1]], axis=0)
        value, slope = cell(previous, cand_pre, gate_pre, rec_gate, rec_cand, bias_gate)
        offset = value - slope * previous
        sweep_a, sweep_b = lax.associative_scan(compose, (slope, offset), axis=0)
        entering = prefix((sweep_a[-1], sweep_b[-1]), "seq", compose, (ones_row, carried * 0.0))
        carried = entering[1]
        state = sweep_a * carried + sweep_b
    state_b = state.astype(jnp.bfloat16)
    partial_sums = jnp.dot(state_b, w_out, preferred_element_type=jnp.float32)
    summed = lax.psum_scatter(partial_sums, "mp", scatter_dimension=1, tiled=True)
    return summed.astype(jnp.bfloat16)


def solution(mesh):
    placed = (
        P("seq", "mp"),
        P(),
        P("seq", "mp"),
        P("seq", "mp"),
        P("mp"),
        P("mp"),
        P("mp"),
        P("mp", None),
    )
    return jax.shard_map(
        per_device, mesh=mesh, in_specs=placed, out_specs=P("seq", "mp"), check_vma=False
    )
```

profile of v0, /device:TPU:0, one launch (start us, length us, event | category | flops | bytes accessed | tf_op | source)
XLA Modules:
  0.0 296.8 jit_solution(11191967048189579970)
XLA Ops:
  6.5 0.7 all-gather.10.cloned.1.call-update
  8.8 30.8 %all-gather.10.cloned.1.call-done = bf16[128,4096]{1,0:T(8,128)(2,1)} async-done(((bf16[128,1024]{1,0:T(8,128)(2,1)}), bf16[128,4096]{1,0:T(8,128)(2,1)}) %all-gather.10.cloned.1.call-update) | async-done | bytes 1048592 | tf_op jit(solution)/shard_map/all_gather | solution.py:42
  39.6 1.5 fusion
  41.2 54.0 %all-gather.12.cloned.1.call-done = bf16[4096,1024]{1,0:T(8,128)(2,1)} async-done(((bf16[512,1024]{1,0:T(8,128)(2,1)}), bf16[4096,1024]{1,0:T(8,128)(2,1)}) %all-gather.12.cloned.1.call-update) | async-done | bytes 8388624 | tf_op jit(solution)/shard_map/all_gather | solution.py:53
  95.2 5.0 %fusion.26 = f32[128,1024]{1,0:T(8,128)S(1)} fusion(bf16[4096,1024]{1,0:T(8,128)(2,1)} %all-gather.12.cloned.1.call-done, bf16[128,4096]{1,0:T(8,128)(2,1)} %all-gather.10.cloned.1.call-done, f32[4096]{0:T(1024)S(1)} %copy-done.5, f32[128]{0:T(128)S(1)} %add_rsqrt_fusion), kind=kOutput, calls=%fused_computation.56 | convolution fusion | flops 1075838976 | bytes 9978368 | tf_op jit(solution)/shard_map/dot_general | solution.py:51
  100.2 51.2 %all-gather.14.cloned.1.call-done = bf16[4096,1024]{1,0:T(8,128)(2,1)} async-done(((bf16[512,1024]{1,0:T(8,128)(2,1)}), bf16[4096,1024]{1,0:T(8,128)(2,1)}) %all-gather.14.cloned.1.call-update) | async-done | bytes 8388624 | tf_op jit(solution)/shard_map/all_gather | solution.py:48
  151.4 5.1 %fusion.6 = (f32[128,1024]{1,0:T(8,128)S(1)}, f32[128,1024]{1,0:T(8,128)S(1)}, f32[128,1024]{1,0:T(8,128)S(1)}) fusion(f32[1024]{0:T(1024)S(1)} %copy-done.6, f32[1024]{0:T(1024)S(1)} %get-tuple-element.441, f32[1024]{0:T(1024)S(1)} %copy-done.7, f32[1024]{0:T(1024)S(1)} %copy-done.8, f32[128,1024]{1,0:T(8,128)S(1)} %fusion.26, ...), kind=kOutput, calls=%fused_computation.26 | convolution fusion | flops 1078722560 | bytes 11571712 | tf_op jit(solution)/shard_map/dot_general | solution.py:46
  156.9 0.8 slice.660
  157.7 1.0 fusion.59
  161.4 0.8 add.628
  162.2 0.8 add_multiply_fusion.5
  163.1 1.7 pad.271
  164.9 1.7 pad.285
  166.7 0.8 add_bitcast_fusion.4
  167.5 9.1 %all-gather.1 = f32[8,1,1024]{2,1,0:T(1,128)S(1)} all-gather(f32[1,1,1024]{2,1,0:T(1,128)S(1)} %add_bitcast_fusion.4), channel_id=1, replica_groups=mesh['seq'=8,'mp'=4] {'seq'}, dimensions={0}, use_global_device_ids=true | all-gather | bytes 36864 | tf_op jit(solution)/shard_map/all_gather | solution.py:11
  176.6 0.8 add_bitcast_fusion.5
  177.4 8.2 %all-gather = f32[8,1,1024]{2,1,0:T(1,128)S(1)} all-gather(f32[1,1,1024]{2,1,0:T(1,128)S(1)} %add_bitcast_fusion.5), channel_id=1, replica_groups=mesh['seq'=8,'mp'=4] {'seq'}, dimensions={0}, use_global_device_ids=true | all-gather | bytes 36864 | tf_op jit(solution)/shard_map/all_gather | solution.py:11
  187.1 0.8 slice.727
  187.9 1.0 fusion.58
  191.7 0.8 add.663
  192.5 0.8 add_multiply_fusion.3
  193.3 1.7 pad.299
  195.1 1.7 pad.313
  197.0 0.8 add_bitcast_fusion.2
  197.7 9.2 %all-gather.3 = f32[8,1,1024]{2,1,0:T(1,128)S(1)} all-gather(f32[1,1,1024]{2,1,0:T(1,128)S(1)} %add_bitcast_fusion.2), channel_id=1, replica_groups=mesh['seq'=8,'mp'=4] {'seq'}, dimensions={0}, use_global_device_ids=true | all-gather | bytes 36864 | tf_op jit(solution)/shard_map/all_gather | solution.py:11
  207.0 0.8 add_bitcast_fusion.3
  207.8 8.2 %all-gather.2 = f32[8,1,1024]{2,1,0:T(1,128)S(1)} all-gather(f32[1,1,1024]{2,1,0:T(1,128)S(1)} %add_bitcast_fusion.3), channel_id=1, replica_groups=mesh['seq'=8,'mp'=4] {'seq'}, dimensions={0}, use_global_device_ids=true | all-gather | bytes 36864 | tf_op jit(solution)/shard_map/all_gather | solution.py:11
  220.9 9.1 %all-gather.5 = f32[8,1,1024]{2,1,0:T(1,128)S(1)} all-gather(f32[1,1,1024]{2,1,0:T(1,128)S(1)} %add_bitcast_fusion), channel_id=1, replica_groups=mesh['seq'=8,'mp'=4] {'seq'}, dimensions={0}, use_global_device_ids=true | all-gather | bytes 36864 | tf_op jit(solution)/shard_map/all_gather | solution.py:11
  230.1 8.2 %all-gather.4 = f32[8,1,1024]{2,1,0:T(1,128)S(1)} all-gather(f32[1,1,1024]{2,1,0:T(1,128)S(1)} %add_bitcast_fusion.1), channel_id=1, replica_groups=mesh['seq'=8,'mp'=4] {'seq'}, dimensions={0}, use_global_device_ids=true | all-gather | bytes 36864 | tf_op jit(solution)/shard_map/all_gather | solution.py:11
  238.7 6.1 %fusion.28 = f32[128,4096]{1,0:T(8,128)} fusion(bf16[1024,4096]{1,0:T(8,128)(2,1)} %param.21, f32[128,1024]{1,0:T(8,128)S(1)} %pad.341, f32[128,1024]{1,0:T(8,128)S(1)} %pad.342, f32[128,1024]{1,0:T(8,128)S(1)} %pad.327, f32[128,1024]{1,0:T(8,128)S(1)} %pad.328, f32[1024]{0:T(1024)S(1)} %get-tuple-element.289), kind=kOutput, calls=%fused_computation.57 | convolution fusion | flops 1074397184 | bytes 12587008 | tf_op jit(solution)/shard_map/dot_general | solution.py:68
  244.8 43.8 %reduce-scatter.2.cloned.1.call-done = f32[128,1024]{1,0:T(8,128)} async-done(((f32[128,4096]{1,0:T(8,128)}), f32[128,1024]{1,0:T(8,128)}) %reduce-scatter.2.cloned.1.call-update) | async-done | bytes 524304 | tf_op jit(solution)/shard_map/reduce_scatter | solution.py:69
  288.5 1.8 convert_element_type.15
  (394 shorter events, 13.8 us)
Async XLA Ops:
  6.5 2.3 copy-start.7
  6.5 2.3 copy-start.6
  6.5 88.7 %copy-start.5 = (f32[4096]{0:T(1024)S(1)}, f32[4096]{0:T(1024)}, u32[]{:S(2)}) copy-start(f32[4096]{0:T(1024)} %param.15) | copy-start | bytes 49156
  6.5 33.1 %all-gather.10.cloned.1.call-start = ((), (), s32[]{:S(2)}) async-start(), calls=%async_computation.1 | async-start | bytes 1310720 | tf_op jit(solution)/shard_map/all_gather | solution.py:42
  7.3 87.9 %all-gather.12.cloned.1.call-start = ((), (), s32[]{:S(2)}) async-start(), calls=%async_computation.2 | async-start | bytes 9437184 | tf_op jit(solution)/shard_map/all_gather | solution.py:53
  8.0 143.4 %all-gather.14.cloned.1.call-start = ((), (), s32[]{:S(2)}) async-start(), calls=%async_computation.3 | async-start | bytes 9437184 | tf_op jit(solution)/shard_map/all_gather | solution.py:48
  8.7 279.8 %reduce-scatter.2.cloned.1.call-start = ((), (), s32[]{:S(2)}) async-start(), calls=%async_computation.4 | async-start | bytes 2621440 | tf_op jit(solution)/shard_map/reduce_scatter | solution.py:69
  41.2 110.2 %copy-start = (bf16[128,4096]{1,0:T(8,128)(2,1)S(1)}, bf16[128,4096]{1,0:T(8,128)(2,1)}, u32[]{:S(2)}) copy-start(bf16[128,4096]{1,0:T(8,128)(2,1)} %all-gather.10.cloned.1.call-done) | copy-start | bytes 3145732
  41.2 110.2 %copy-start.8 = (f32[1024]{0:T(1024)S(1)}, f32[1024]{0:T(1024)}, u32[]{:S(2)}) copy-start(f32[1024]{0:T(1024)} %param.20) | copy-start | bytes 12292
  163.0 1.8 copy-start.3
  163.0 3.6 %copy-start.1 = (f32[64,1024]{1,0:T(8,128)S(1)}, f32[64,1024]{1,0:T(8,128)}, u32[]{:S(2)}) copy-start(f32[64,1024]{1,0:T(8,128)} %add.628) | copy-start | bytes 786436
  193.3 1.8 copy-start.4
  193.3 3.6 %copy-start.2 = (f32[64,1024]{1,0:T(8,128)S(1)}, f32[64,1024]{1,0:T(8,128)}, u32[]{:S(2)}) copy-start(f32[64,1024]{1,0:T(8,128)} %add.663) | copy-start | bytes 786436
Sparse Core Ops, SparseCore 0:
  8.9 30.6 all-gather.9
  41.5 53.6 all-gather.11
  97.1 54.2 all-gather.13
  244.9 43.6 reduce-scatter.1
where the time goes:
time: 298 us; the launch traced here: 297 us
  waiting for transfers between devices  182 us (61%)
  blocking collectives  51.9 us (17%)
  local copies, waits for them, and re-layouts  16.1 us (5%)
  matrix products  16.1 us (5%)
  between operations  15.1 us (5%)
  other arithmetic  15 us (5%)
    all_gather x1, waiting for transfers between devices, per_device(): lax.all_gather(w_gate, 'seq', axis=0, tiled=True)  54 us
    all_gather x6, blocking collectives, prefix(): pieces = jax.tree.map(lambda part: lax.all_gather(part, axis), value)  51.9 us
    all_gather x1, waiting for transfers between devices, per_device(): lax.all_gather(w_cand, 'seq', axis=0, tiled=True)  51.2 us
    reduce_scatter x1, waiting for transfers between devices, per_device(): lax.psum_scatter(partial_sums, 'mp', scatter_dimension=1, tiled=True)  43.8 us
    all_gather x1, waiting for transfers between devices, per_device(): whole = lax.all_gather(tokens, 'mp', axis=1, tiled=True)  30.8 us
    pad x68, local copies, waits for them, and re-layouts, per_device(): sweep_a, sweep_b = lax.associative_scan(compose, (slope, offset), axis=0)  8.35 us
    slice x132, local copies, waits for them, and re-layouts, per_device(): sweep_a, sweep_b = lax.associative_scan(compose, (slope, offset), axis=0)  6.86 us
    dot_general x1, matrix products, per_device(): partial_sums = jnp.dot(state_b, w_out, preferred_element_type=jnp.float32)  6.06 us
  transfers between devices with their start and end apart: 4, of which 4 were waited for; matrix products, arithmetic and copies ran while one was open for 2% of the time, Pallas kernels for 0%

commit v1 on v0

--- a/solution.py
+++ b/solution.py
@@ -1,6 +1,10 @@
+import functools
+
 import jax
 import jax.numpy as jnp
 from jax import lax
+from jax.experimental import pallas as pl
+from jax.experimental.pallas import tpu as pltpu
 from jax.sharding import PartitionSpec as P
 
 NEWTON = 3
@@ -70,6 +74,382 @@
     return summed.astype(jnp.bfloat16)
 
 
+CORES = 2
+SUBLANES = 8
+LANES = 128
+MESH = pl.DeviceIdType.MESH
+
+
+def fused_kernel(
+    n_seq,
+    n_mp,
+    tok_ref,
+    gain_ref,
+    wc_hbm,
+    wg_hbm,
+    rg_ref,
+    rc_ref,
+    bg_ref,
+    wo_hbm,
+    out_ref,
+    raw,
+    nsend,
+    xk,
+    wk,
+    wo,
+    own,
+    psend,
+    precv,
+    cand_n,
+    gate_n,
+    sweep_a,
+    sweep_b,
+    carry,
+    ssend,
+    sall,
+    pout,
+    osend,
+    orecv,
+    w_loc,
+    w_snd,
+    w_rcv,
+    wo_sem,
+    z_snd,
+    z_rcv,
+    k_snd,
+    k_rcv,
+    f_snd,
+    p_snd,
+    p_rcv,
+    s_snd,
+    s_rcv,
+    o_snd,
+    o_rcv,
+):
+    s, m = (lax.axis_index("seq"), lax.axis_index("mp"))
+    n_chip = n_seq // CORES
+    c, r = (s // CORES, s % CORES)
+    mate = c * CORES + (1 - r)
+    rows = tok_ref.shape[0]
+    tokens = rows * n_seq
+    k_own = wc_hbm.shape[0]
+    width = raw.shape[2]
+    q = r * n_chip + c
+
+    def remote(src, dst, snd, rcv, **where):
+        return pltpu.make_async_remote_copy(
+            src_ref=src, dst_ref=dst, send_sem=snd, recv_sem=rcv, device_id=where, device_id_type=MESH
+        )
+
+    def barrier():
+        sem = pltpu.get_barrier_semaphore()
+        for o in range(1, n_seq):
+            pl.semaphore_signal(sem, inc=1, device_id={"seq": (s + o) % n_seq}, device_id_type=MESH)
+        for o in range(1, n_mp):
+            pl.semaphore_signal(sem, inc=1, device_id={"mp": (m + o) % n_mp}, device_id_type=MESH)
+        pl.semaphore_wait(sem, n_seq + n_mp - 2)
+
+    def w_piece(hbm, core, chip):
+        return hbm.at[:, pl.ds(pl.multiple_of((core * n_chip + chip) * LANES, LANES), LANES)]
+
+    def w_place(i, chip, core):
+        return wk.at[chip, pl.ds(pl.multiple_of(core * k_own, k_own), k_own), pl.ds(i * LANES, LANES)]
+
+    local = [
+        pltpu.make_async_copy(w_piece(hbm, r, chip), w_place(i, chip, r), w_loc.at[i, chip])
+        for chip in range(n_chip)
+        for i, hbm in enumerate((wc_hbm, wg_hbm))
+    ]
+    wo_copy = pltpu.make_async_copy(wo_hbm, wo, wo_sem)
+    for copy in local:
+        copy.start()
+    barrier()
+
+    def right_copy(src, b, k):
+        return remote(src, raw.at[b], z_snd.at[0, k], z_rcv.at[b], mp=(m + 1) % n_mp)
+
+    def left_copy(src, b, k):
+        return remote(src, raw.at[b], z_snd.at[1, k], z_rcv.at[b], mp=(m + n_mp - 1) % n_mp)
+
+    @pl.when(m < n_mp - 1)
+    def _():
+        right_copy(tok_ref, m, 0).start()
+
+    @pl.when(m > 0)
+    def _():
+        left_copy(tok_ref, m, 0).start()
+
+    w_out_copies = [
+        remote(w_piece(hbm, 1 - r, chip), w_place(i, chip, r), w_snd.at[i, chip], w_rcv.at[i, chip], seq=mate)
+        for chip in range(n_chip)
+        for i, hbm in enumerate((wc_hbm, wg_hbm))
+    ]
+    for copy in w_out_copies:
+        copy.start()
+    wo_copy.start()
+
+    raw[pl.ds(m, 1)] = tok_ref[...][None]
+    for k in range(1, n_mp):
+
+        @pl.when(m - k >= 0)
+        def _():
+            b = m - k
+            right_copy(raw.at[b], b, 0).wait_recv()
+
+            @pl.when(m < n_mp - 1)
+            def _():
+                right_copy(raw.at[b], b, k).start()
+
+        @pl.when(m + k <= n_mp - 1)
+        def _():
+            b = m + k
+            left_copy(raw.at[b], b, 0).wait_recv()
+
+            @pl.when(m > 0)
+            def _():
+                left_copy(raw.at[b], b, k).start()
+
+    group = 16
+
+    @pl.loop(0, rows // group)
+    def _(i):
+        at = pl.ds(pl.multiple_of(i * group, group), group)
+        total = jnp.zeros((group, 1), jnp.float32)
+        for b in range(n_mp):
+            wide = raw[b, at, :].astype(jnp.float32)
+            total = total + jnp.sum(wide * wide, axis=1, keepdims=True)
+        factor = lax.rsqrt(total / (width * n_mp) + 1e-05)
+        for b in range(n_mp):
+            wide = raw[b, at, :].astype(jnp.float32)
+            nsend[b, at, :] = (wide * factor * gain_ref[:, b * width : (b + 1) * width]).astype(jnp.bfloat16)
+
+    def block(seq):
+        return pl.ds(pl.multiple_of(seq * rows, rows), rows)
+
+    scatter = []
+    for o in range(1, n_chip):
+        chip = (c + o) % n_chip
+        scatter.append(
+            remote(nsend.at[chip], xk.at[block(s)], k_snd.at[o], k_rcv.at[s], seq=chip * CORES + r)
+        )
+    scatter.append(remote(nsend.at[c], xk.at[block(s)], k_snd.at[0], k_rcv.at[s], seq=mate))
+    for copy in scatter:
+        copy.start()
+    xk[block(s), :] = nsend[pl.ds(c, 1)].reshape(rows, width)
+    forward = []
+    for o in range(1, n_chip):
+        there = ((c + n_chip - o) % n_chip) * CORES + r
+        remote(nsend.at[c], xk.at[block(there)], k_snd.at[0], k_rcv.at[there], seq=mate).wait_recv()
+        copy = remote(xk.at[block(there)], xk.at[block(there)], f_snd.at[o], k_rcv.at[there], seq=mate)
+        copy.start()
+        forward.append(copy)
+    for copy in local:
+        copy.wait()
+    for copy in w_out_copies:
+        copy.wait()
+    for o in range(n_chip):
+        there = ((c + n_chip - o) % n_chip) * CORES + (1 - r)
+        remote(nsend.at[c], xk.at[block(there)], k_snd.at[0], k_rcv.at[there], seq=mate).wait_recv()
+
+    step = 256
+    partial = []
+    for o in list(range(1, n_chip)) + [0]:
+        chip = (c + o) % n_chip
+
+        @pl.loop(0, tokens // step)
+        def _(i):
+            at = pl.ds(pl.multiple_of(i * step, step), step)
+            value = jnp.dot(xk[at, :], wk[chip], preferred_element_type=jnp.float32)
+            if o == 0:
+                own[at, :] = value
+            else:
+                psend[o - 1, at, :] = value.astype(jnp.bfloat16)
+
+        if o > 0:
+            copy = remote(
+                psend.at[o - 1], precv.at[o - 1], p_snd.at[o - 1], p_rcv.at[o - 1], seq=chip * CORES + r
+            )
+            copy.start()
+            partial.append(copy)
+    bias = bg_ref[pl.ds(q, 1), :]
+    rec_gate = rg_ref[pl.ds(q, 1), :]
+    rec_cand = rc_ref[pl.ds(q, 1), :]
+    for copy in partial:
+        copy.wait_recv()
+
+    @pl.loop(0, tokens // group)
+    def _(i):
+        at = pl.ds(pl.multiple_of(i * group, group), group)
+        value = own[at, :]
+        for o in range(n_chip - 1):
+            value = value + precv[o, at, :].astype(jnp.float32)
+        cand_n[at, :] = value[:, :LANES]
+        gate_n[at, :] = value[:, LANES:] + bias
+
+    for newton_step in range(NEWTON):
+        entering = jnp.zeros((n_seq, LANES), jnp.float32) if newton_step == 0 else carry[...]
+
+        def lap(j, held):
+            previous, a, b = held
+            cand_pre = cand_n[pl.ds(j, n_seq, stride=rows), :]
+            gate_pre = gate_n[pl.ds(j, n_seq, stride=rows), :]
+            value, slope = cell(previous, cand_pre, gate_pre, rec_gate, rec_cand, 0.0)
+            offset = value - slope * previous
+            if newton_step > 0:
+                previous = sweep_a[j] * entering + sweep_b[j]
+            a, b = (slope * a, slope * b + offset)
+            sweep_a[j] = a
+            sweep_b[j] = b
+            return (previous, a, b)
+
+        zero = jnp.zeros((n_seq, LANES), jnp.float32)
+        _, a, b = lax.fori_loop(0, rows, lap, (entering, zero + 1.0, zero), unroll=8)
+        state = jnp.zeros((1, LANES), jnp.float32)
+        for i in range(n_seq):
+            carry[i : i + 1, :] = state
+            state = a[i : i + 1, :] * state + b[i : i + 1, :]
+    entering = carry[...]
+
+    @pl.loop(0, rows, unroll=8)
+    def _(j):
+        cand_n[pl.ds(j, n_seq, stride=rows), :] = sweep_a[j] * entering + sweep_b[j]
+
+    for i in range(n_seq):
+        ssend[i] = cand_n[i * rows : (i + 1) * rows, :].astype(jnp.bfloat16)
+    lane = pl.ds(pl.multiple_of(q * LANES, LANES), LANES)
+    spread = []
+    for o in range(1, n_seq):
+        there = (s + o) % n_seq
+        copy = remote(ssend.at[there], sall.at[:, lane], s_snd.at[o], s_rcv.at[o], seq=there)
+        copy.start()
+        spread.append(copy)
+    sall[:, lane] = ssend[pl.ds(s, 1)].reshape(rows, LANES)
+    wo_copy.wait()
+    for copy in spread:
+        copy.wait_recv()
+
+    cols = out_ref.shape[1]
+    for d in range(n_mp):
+        pout[d] = jnp.dot(sall[...], wo[:, d * cols : (d + 1) * cols], preferred_element_type=jnp.float32)
+
+    def hop(side, d):
+        there = (m + 1) % n_mp if side == 0 else (m + n_mp - 1) % n_mp
+        return remote(osend.at[d], orecv.at[side, d], o_snd.at[d], o_rcv.at[side, d], mp=there)
+
+    for k in range(n_mp - 1, 0, -1):
+        for side, sign in ((0, 1), (1, -1)):
+            d = m + sign * k
+            inside = (d <= n_mp - 1) if side == 0 else (d >= 0)
+            first = (m == 0) if side == 0 else (m == n_mp - 1)
+
+            @pl.when(inside & first)
+            def _():
+                osend[d] = pout[d].astype(jnp.bfloat16)
+                hop(side, d).start()
+
+            @pl.when(inside & jnp.logical_not(first))
+            def _():
+                hop(side, d).wait_recv()
+                osend[d] = (pout[d] + orecv[side, d].astype(jnp.float32)).astype(jnp.bfloat16)
+                hop(side, d).start()
+
+    @pl.when(m > 0)
+    def _():
+        hop(0, m).wait_recv()
+        pout[m] = pout[m] + orecv[0, m].astype(jnp.float32)
+
+    @pl.when(m < n_mp - 1)
+    def _():
+        hop(1, m).wait_recv()
+        pout[m] = pout[m] + orecv[1, m].astype(jnp.float32)
+
+    out_ref[...] = pout[m].astype(jnp.bfloat16)
+
+    for k in range(n_mp - 1):
+
+        @pl.when((m < n_mp - 1) & (m - k >= 0))
+        def _():
+            right_copy(raw.at[m - k], m - k, k).wait_send()
+
+        @pl.when((m > 0) & (m + k <= n_mp - 1))
+        def _():
+            left_copy(raw.at[m + k], m + k, k).wait_send()
+
+    for copy in scatter + forward + partial + spread:
+        copy.wait_send()
+    for d in range(n_mp):
+
+        @pl.when(d != m)
+        def _():
+            hop(0, d).wait_send()
+
+
+def fused(n_seq, n_mp, tokens, norm_gain, w_cand, w_gate, rec_gate, rec_cand, bias_gate, w_out):
+    rows, width = tokens.shape
+    k_own, channels = w_cand.shape
+    n_chip = n_seq // CORES
+    length = rows * n_seq
+    bf16, f32 = (jnp.bfloat16, jnp.float32)
+    vmem, dma = (pltpu.VMEM, pltpu.SemaphoreType.DMA)
+    whole = pl.BlockSpec(memory_space=pltpu.VMEM)
+    far = pl.BlockSpec(memory_space=pl.ANY)
+    per_channel = [part.reshape(n_seq, LANES) for part in (rec_gate, rec_cand, bias_gate)]
+    return pl.pallas_call(
+        functools.partial(fused_kernel, n_seq, n_mp),
+        out_shape=jax.ShapeDtypeStruct((rows, width), bf16),
+        in_specs=[whole, whole, far, far, whole, whole, whole, far],
+        out_specs=whole,
+        scratch_shapes=[
+            vmem((n_mp, rows, width), bf16),
+            vmem((n_chip, rows, width), bf16),
+            vmem((length, width), bf16),
+            vmem((n_chip, k_own * CORES, 2 * LANES), bf16),
+            vmem(w_out.shape, bf16),
+            vmem((length, 2 * LANES), f32),
+            vmem((n_chip - 1, length, 2 * LANES), bf16),
+            vmem((n_chip - 1, length, 2 * LANES), bf16),
+            vmem((length, LANES), f32),
+            vmem((length, LANES), f32),
+            vmem((rows, n_seq, LANES), f32),
+            vmem((rows, n_seq, LANES), f32),
+            vmem((n_seq, LANES), f32),
+            vmem((n_seq, rows, LANES), bf16),
+            vmem((rows, channels), bf16),
+            vmem((n_mp, rows, width), f32),
+            vmem((n_mp, rows, width), bf16),
+            vmem((2, n_mp, rows, width), bf16),
+            dma((2, n_chip)),
+            dma((2, n_chip)),
+            dma((2, n_chip)),
+            dma,
+            dma((2, n_mp)),
+            dma((n_mp,)),
+            dma((n_chip,)),
+            dma((n_seq,)),
+            dma((n_chip,)),
+            dma((n_chip,)),
+            dma((n_chip,)),
+            dma((n_seq,)),
+            dma((n_seq,)),
+            dma((n_mp,)),
+            dma((2, n_mp)),
+        ],
+        compiler_params=pltpu.CompilerParams(collective_id=0, has_side_effects=True),
+    )(tokens, norm_gain.reshape(1, -1), w_cand, w_gate, *per_channel, w_out)
+
+
+def layer(n_seq, n_mp, *args):
+    tokens, w_cand = (args[0], args[2])
+    fits = (
+        n_seq == SUBLANES
+        and n_seq // CORES == n_mp
+        and w_cand.shape[1] == n_seq * LANES
+        and tokens.shape[0] % LANES == 0
+        and tokens.shape[1] % LANES == 0
+    )
+    return fused(n_seq, n_mp, *args) if fits else per_device(*args)
+
+
 def solution(mesh):
     placed = (
         P("seq", "mp"),
@@ -82,5 +462,5 @@
         P("mp", None),
     )
     return jax.shard_map(
-        per_device, mesh=mesh, in_specs=placed, out_specs=P("seq", "mp"), check_vma=False
-    )
+        functools.partial(layer, mesh.shape["seq"], mesh.shape["mp"]), mesh=mesh, in_specs=placed, out_specs=P("seq", "mp"), check_vma=False
+    )

time: 298 us -> 102 us (0.34)
  waiting for transfers between devices: 182 us -> 0 us
  Pallas kernels: 0 us -> 99.8 us
  blocking collectives: 51.9 us -> 0 us
  matrix products: 16.1 us -> 0 us
  between operations: 15.1 us -> 0.01 us
  other arithmetic: 15 us -> 0 us
  local copies, waits for them, and re-layouts: 16.1 us -> 1.67 us
    all_gather x3 -> x0, waiting for transfers between devices: 136 us -> none  [the longest x1 54 us: per_device(): lax.all_gather(w_gate, 'seq', axis=0, tiled=True)]
    pallas_call x0 -> x1, Pallas kernels: none -> 99.8 us  [fused(): pl.pallas_call(functools.partial(fused_kernel, n_seq, n_mp), out_shape=ja...]
    all_gather x6 -> x0, blocking collectives: 51.9 us -> none  [prefix(): pieces = jax.tree.map(lambda part: lax.all_gather(part, axis), value)]
    reduce_scatter x1 -> x0, waiting for transfers between devices: 43.8 us -> none  [per_device(): lax.psum_scatter(partial_sums, 'mp', scatter_dimension=1, tiled=True)]
    dot_general x3 -> x0, matrix products: 16.1 us -> none  [the longest x1 6.06 us: per_device(): partial_sums = jnp.dot(state_b, w_out, preferred_element_type=jnp.float32)]
    pad x68 -> x0, local copies, waits for them, and re-layouts: 8.35 us -> none  [per_device(): sweep_a, sweep_b = lax.associative_scan(compose, (slope, offset), axis=0)]
    slice x136 -> x0, local copies, waits for them, and re-layouts: 7.13 us -> none  [the longest x132 6.86 us: per_device(): sweep_a, sweep_b = lax.associative_scan(compose, (slope, offset), axis=0)]
    mul x39 -> x0, other arithmetic: 4.43 us -> none  [the longest x36 4.42 us: compose(): return (later[0] * earlier[0], later[0] * earlier[1] + later[1])]
  transfers between devices with their start and end apart: 4 -> 0, of which waited for: 4 -> 0; matrix products, arithmetic and copies ran while one was open for 2% -> 0% of each run, Pallas kernels for 0% -> 0%
where the time goes in v1:
time: 102 us
  Pallas kernels  99.8 us (98%)
  local copies, waits for them, and re-layouts  1.67 us (2%)
    pallas_call x1, Pallas kernels, fused(): pl.pallas_call(functools.partial(fused_kernel, n_seq, n_mp), out_shape=ja...  99.8 us

profile of v1, /device:TPU:0, one launch (start us, length us, event | category | flops | bytes accessed | tf_op | source)
XLA Modules:
  0.0 101.5 jit_solution(9430678472409269844)
XLA Ops:
  0.0 99.8 %shard_map.82 = bf16[128,1024]{1,0:T(8,128)(2,1)} custom-call(bf16[128,1024]{1,0:T(8,128)(2,1)} %tok_ref.1, f32[1,4096]{1,0:T(1,128)} %bitcast.4, bf16[512,1024]{1,0:T(8,128)(2,1)} %wc_hbm.1, bf16[512,1024]{1,0:T(8,128)(2,1)} %wg_hbm.1, f32[8,128]{1,0:T(8,128)} %bitcast.5, f32[8,128]{1,0:T(8,128)} %bitcast.6, f32[8,128]{1,0:T(8,128)} %bitcast.7, ...), custom_call_target="tpu_custom_call" | custom-call | tf_op jit(solution)/shard_map/pallas_call | solution.py:397
  99.8 1.7 %copy.10 = bf16[128,1024]{1,0:T(8,128)(2,1)} copy(bf16[128,1024]{1,0:T(8,128)(2,1)} %shard_map.82) | data formatting | bytes 524288

commit v2 on v1

v2 whole, which is shorter than its diff:
```python
import functools

import jax
import jax.numpy as jnp
from jax import lax
from jax.experimental import pallas as pl
from jax.experimental.pallas import tpu as pltpu
from jax.sharding import PartitionSpec as P

NEWTON = 3


def prefix(value, axis, join, neutral):
    count, mine = (lax.axis_size(axis), lax.axis_index(axis))
    pieces = jax.tree.map(lambda part: lax.all_gather(part, axis), value)
    subtotal = jax.tree.map(
        lambda part, zero: jnp.full_like(part, 0) + jnp.asarray(zero, part.dtype), value, neutral
    )

    def lap(position, subtotal):
        longer = join(subtotal, jax.tree.map(lambda part: part[position], pieces))
        return jax.tree.map(lambda new, old: jnp.where(position < mine, new, old), longer, subtotal)

    return lax.fori_loop(0, count - 1, lap, subtotal)


def compose(earlier, later):
    return (later[0] * earlier[0], later[0] * earlier[1] + later[1])


def cell(previous, cand_pre, gate_pre, rec_gate, rec_cand, bias_gate):
    gate = jax.nn.sigmoid(gate_pre + rec_gate * previous + bias_gate)
    cand = jnp.tanh(cand_pre + rec_cand * previous)
    value = gate * previous + (1.0 - gate) * cand
    slope = (
        gate
        + gate * (1.0 - gate) * rec_gate * (previous - cand)
        + (1.0 - gate) * (1.0 - cand * cand) * rec_cand
    )
    return (value, slope)


def per_device(tokens, norm_gain, w_cand, w_gate, rec_gate, rec_cand, bias_gate, w_out):
    tok_rows = tokens.shape[0]
    channels = w_cand.shape[1]
    whole = lax.all_gather(tokens, "mp", axis=1, tiled=True)
    wide = whole.astype(jnp.float32)
    factor = lax.rsqrt(jnp.mean(wide * wide, axis=1, keepdims=True) + 1e-05)
    normed = (wide * factor * norm_gain).astype(jnp.bfloat16)
    cand_pre = jnp.dot(
        normed,
        lax.all_gather(w_cand, "seq", axis=0, tiled=True),
        preferred_element_type=jnp.float32,
    )
    gate_pre = jnp.dot(
        normed,
        lax.all_gather(w_gate, "seq", axis=0, tiled=True),
        preferred_element_type=jnp.float32,
    )
    state = jnp.zeros((tok_rows, channels), jnp.float32)
    carried = jnp.zeros((channels,), jnp.float32)
    ones_row = jnp.ones((channels,), jnp.float32)
    for newton_step in range(NEWTON):
        previous = jnp.concatenate([carried[None, :], state[:-1]], axis=0)
        value, slope = cell(previous, cand_pre, gate_pre, rec_gate, rec_cand, bias_gate)
        offset = value - slope * previous
        sweep_a, sweep_b = lax.associative_scan(compose, (slope, offset), axis=0)
        entering = prefix((sweep_a[-1], sweep_b[-1]), "seq", compose, (ones_row, carried * 0.0))
        carried = entering[1]
        state = sweep_a * carried + sweep_b
    state_b = state.astype(jnp.bfloat16)
    partial_sums = jnp.dot(state_b, w_out, preferred_element_type=jnp.float32)
    summed = lax.psum_scatter(partial_sums, "mp", scatter_dimension=1, tiled=True)
    return summed.astype(jnp.bfloat16)


CORES = 2
SUBLANES = 8
LANES = 128
PIECES = 4
HALVES = 2
GROUP = 16
MESH = pl.DeviceIdType.MESH


def fused_kernel(
    n_seq,
    n_mp,
    tok_ref,
    gain_ref,
    wc_hbm,
    wg_hbm,
    rg_ref,
    rc_ref,
    bg_ref,
    wo_hbm,
    out_ref,
    raw,
    xk,
    xn,
    sq_own,
    sq_all,
    f_own,
    f_all,
    f_col,
    wk,
    wo,
    own,
    psend,
    precv,
    cand_n,
    gate_n,
    sweep_a,
    sweep_b,
    carry,
    ssend,
    sall,
    pout,
    osend,
    orecv,
    w_loc,
    w_snd,
    w_rcv,
    wo_sem,
    z_snd,
    z_rcv,
    k_snd,
    k_rcv,
    f_snd,
    q_snd,
    q_rcv,
    g_snd,
    g_rcv,
    p_snd,
    p_rcv,
    s_snd,
    s_rcv,
    o_snd,
    o_rcv,
):
    s, m = (lax.axis_index("seq"), lax.axis_index("mp"))
    n_chip = n_seq // CORES
    c, r = (s // CORES, s % CORES)
    mate = c * CORES + (1 - r)
    rows = tok_ref.shape[0]
    tokens = rows * n_seq
    k_own = wc_hbm.shape[0]
    width = raw.shape[2]
    q = r * n_chip + c

    def remote(src, dst, snd, rcv, **where):
        return pltpu.make_async_remote_copy(
            src_ref=src, dst_ref=dst, send_sem=snd, recv_sem=rcv, device_id=where, device_id_type=MESH
        )

    def barrier():
        sem = pltpu.get_barrier_semaphore()
        for o in range(1, n_seq):
            pl.semaphore_signal(sem, inc=1, device_id={"seq": (s + o) % n_seq}, device_id_type=MESH)
        for o in range(1, n_mp):
            pl.semaphore_signal(sem, inc=1, device_id={"mp": (m + o) % n_mp}, device_id_type=MESH)
        pl.semaphore_wait(sem, n_seq + n_mp - 2)

    def w_piece(hbm, core, chip):
        return hbm.at[:, pl.ds(pl.multiple_of((core * n_chip + chip) * LANES, LANES), LANES)]

    def w_place(i, chip, core):
        return wk.at[chip, pl.ds(pl.multiple_of(core * k_own, k_own), k_own), pl.ds(i * LANES, LANES)]

    local = [
        pltpu.make_async_copy(w_piece(hbm, r, chip), w_place(i, chip, r), w_loc.at[i, chip])
        for chip in range(n_chip)
        for i, hbm in enumerate((wc_hbm, wg_hbm))
    ]
    wo_copy = pltpu.make_async_copy(wo_hbm, wo, wo_sem)
    for copy in local:
        copy.start()
    barrier()

    part = rows // PIECES

    def piece(p):
        return pl.ds(p * part, part)

    def place(p, seq):
        return pl.ds(pl.multiple_of((p * n_seq + seq) * part, part), part)

    def z_copy(side, src, b, p, k):
        there = (m + 1) % n_mp if side == 0 else (m + n_mp - 1) % n_mp
        return remote(src, raw.at[b, piece(p)], z_snd.at[side, k, p], z_rcv.at[b, p], mp=there)

    def not_last(side):
        return m < n_mp - 1 if side == 0 else m > 0

    def plane_copy(src, b, p):
        seq = jnp.where(b == c, mate, b * CORES + r)
        return remote(src, xk.at[place(p, s)], k_snd.at[b, p], k_rcv.at[p, s], seq=seq)

    def send_own(p):
        mine = tok_ref.at[piece(p)]
        for side in range(2):

            @pl.when(not_last(side))
            def _():
                z_copy(side, mine, m, p, 0).start()

        plane_copy(mine, m, p).start()

        @pl.when(m == c)
        def _():
            xk[place(p, s), :] = tok_ref[piece(p), :]

    def pass_on(p, k):
        for side, sign in ((0, -1), (1, 1)):
            b = m + sign * k

            @pl.when((b >= 0) & (b <= n_mp - 1))
            def _():
                here = raw.at[b, piece(p)]
                z_copy(side, here, b, p, 0).wait_recv()

                @pl.when(not_last(side))
                def _():
                    z_copy(side, here, b, p, k).start()

                plane_copy(here, b, p).start()

                @pl.when(b == c)
                def _():
                    xk[place(p, s), :] = raw[b, piece(p), :]

    for p in range(min(2, PIECES)):
        send_own(p)

    across = lax.broadcasted_iota(jnp.int32, (rows, rows), 0) == lax.broadcasted_iota(
        jnp.int32, (rows, rows), 1
    )
    wide = tok_ref[...].astype(jnp.float32)
    squares = jnp.sum(wide * wide, axis=1, keepdims=True)
    squares = jnp.sum(jnp.where(across, squares, 0.0), axis=0, keepdims=True)
    sq_own[...] = jnp.broadcast_to(squares, sq_own.shape)
    sq_copies = []
    for o in range(1, n_mp):
        copy = remote(sq_own, sq_all.at[o], q_snd.at[o], q_rcv.at[o], mp=(m + o) % n_mp)
        copy.start()
        sq_copies.append(copy)

    w_out_copies = [
        remote(w_piece(hbm, 1 - r, chip), w_place(i, chip, r), w_snd.at[i, chip], w_rcv.at[i, chip], seq=mate)
        for chip in range(n_chip)
        for i, hbm in enumerate((wc_hbm, wg_hbm))
    ]
    for copy in w_out_copies:
        copy.start()
    wo_copy.start()
    gain = gain_ref[pl.ds(c, 1), :]
    bias = bg_ref[pl.ds(q, 1), :]
    rec_gate = rg_ref[pl.ds(q, 1), :]
    rec_cand = rc_ref[pl.ds(q, 1), :]
    tile = n_seq * part
    forward, partial, f_copies = ([], [], [])

    def stage_a(p):
        for k in range(1, n_mp):
            pass_on(p, k)
            if k == 1 and p + 2 < PIECES:
                send_own(p + 2)

    def factors():
        total = sq_own[...]
        for copy in sq_copies:
            copy.wait_recv()
        for o in range(1, n_mp):
            total = total + sq_all[o]
        f_own[...] = lax.rsqrt(total / (width * n_mp) + 1e-05)
        for o in range(1, n_seq):
            copy = remote(f_own, f_all.at[s], g_snd.at[o], g_rcv.at[s], seq=(s + o) % n_seq)
            copy.start()
            f_copies.append(copy)
        f_all[pl.ds(s, 1)] = f_own[...][None]

    def spread_factors():
        for o in range(1, n_seq):
            there = (s + o) % n_seq
            remote(f_own, f_all.at[there], g_snd.at[o], g_rcv.at[there], seq=there).wait_recv()
        for i in range(n_seq):
            row = f_all[i, 0:1, :]
            column = jnp.sum(jnp.where(across, row, 0.0), axis=1, keepdims=True)
            column = jnp.broadcast_to(column, (rows, LANES))
            for p in range(PIECES):
                f_col[(p * n_seq + i) * part : (p * n_seq + i + 1) * part, :] = column[
                    p * part : (p + 1) * part, :
                ]

    def arrived(p, seq):
        remote(tok_ref.at[piece(p)], xk.at[place(p, seq)], k_snd.at[0, p], k_rcv.at[p, seq], seq=mate).wait_recv()

    def stage_b(p):
        for o in range(1, n_chip):
            there = ((c + n_chip - o) % n_chip) * CORES + r
            arrived(p, there)
            copy = remote(
                xk.at[place(p, there)], xk.at[place(p, there)], f_snd.at[o, p], k_rcv.at[p, there], seq=mate
            )
            copy.start()
            forward.append(copy)

    def stage_c(p):
        for o in range(n_chip):
            arrived(p, ((c + n_chip - o) % n_chip) * CORES + (1 - r))

        @pl.loop(0, tile // GROUP)
        def _(i):
            at = pl.ds(pl.multiple_of(i * GROUP, GROUP), GROUP)
            of = pl.ds(pl.multiple_of(p * tile + i * GROUP, GROUP), GROUP)
            xn[at, :] = (xk[of, :].astype(jnp.float32) * f_col[of, 0:1] * gain).astype(jnp.bfloat16)

        at = pl.ds(p * tile, tile)
        for o in list(range(1, n_chip)) + [0]:
            chip = (c + o) % n_chip
            value = jnp.dot(xn[...], wk[chip], preferred_element_type=jnp.float32)
            if o == 0:
                own[at, :] = value
            else:
                psend[o - 1, at, :] = value.astype(jnp.bfloat16)
                copy = remote(
                    psend.at[o - 1, at],
                    precv.at[o - 1, at],
                    p_snd.at[o, p],
                    p_rcv.at[o, p],
                    seq=chip * CORES + r,
                )
                copy.start()
                partial.append(copy)

    for turn in range(PIECES + 2):
        if turn < PIECES:
            stage_a(turn)
        if turn == 0:
            factors()
        if 0 <= turn - 1 < PIECES:
            stage_b(turn - 1)
        if turn == 1:
            spread_factors()
            for copy in local:
                copy.wait()
            for copy in w_out_copies:
                copy.wait()
        if 0 <= turn - 2 < PIECES:
            stage_c(turn - 2)

    def gather_piece(p):
        for copy in partial[p * (n_chip - 1) : (p + 1) * (n_chip - 1)]:
            copy.wait_recv()

        @pl.loop(0, tile // GROUP)
        def _(i):
            at = pl.ds(pl.multiple_of(p * tile + i * GROUP, GROUP), GROUP)
            value = own[at, :]
            for o in range(n_chip - 1):
                value = value + precv[o, at, :].astype(jnp.float32)
            cand_n[at, :] = value[:, :LANES]
            gate_n[at, :] = value[:, LANES:] + bias

    for newton_step in range(NEWTON):
        zero = jnp.zeros((n_seq, LANES), jnp.float32)
        entering = zero if newton_step == 0 else carry[...]
        held = (entering, zero + 1.0, zero)
        for p in range(PIECES):
            if newton_step == 0:
                gather_piece(p)

            def lap(i, held):
                previous, a, b = held
                j = p * part + i
                at = pl.ds(p * tile + i, n_seq, stride=part)
                value, slope = cell(previous, cand_n[at, :], gate_n[at, :], rec_gate, rec_cand, 0.0)
                offset = value - slope * previous
                if newton_step > 0:
                    previous = sweep_a[j] * entering + sweep_b[j]
                a, b = (slope * a, slope * b + offset)
                sweep_a[j] = a
                sweep_b[j] = b
                return (previous, a, b)

            held = lax.fori_loop(0, part, lap, held, unroll=8)
        _, a, b = held
        state = jnp.zeros((1, LANES), jnp.float32)
        for i in range(n_seq):
            carry[i : i + 1, :] = state
            state = a[i : i + 1, :] * state + b[i : i + 1, :]
    entering = carry[...]
    for p in range(PIECES):

        @pl.loop(0, part, unroll=8)
        def _(i):
            j = p * part + i
            cand_n[pl.ds(p * tile + i, n_seq, stride=part), :] = sweep_a[j] * entering + sweep_b[j]

    for i in range(n_seq):
        for p in range(PIECES):
            start = (p * n_seq + i) * part
            ssend[i, p * part : (p + 1) * part, :] = cand_n[start : start + part, :].astype(jnp.bfloat16)
    lane = pl.ds(pl.multiple_of(q * LANES, LANES), LANES)
    spread = []
    for o in range(1, n_seq):
        there = (s + o) % n_seq
        copy = remote(ssend.at[there], sall.at[:, lane], s_snd.at[o], s_rcv.at[o], seq=there)
        copy.start()
        spread.append(copy)
    sall[:, lane] = ssend[pl.ds(s, 1)].reshape(rows, LANES)
    wo_copy.wait()
    for copy in spread:
        copy.wait_recv()

    cols = out_ref.shape[1]
    half = rows // HALVES

    def hop(side, d, h):
        there = (m + 1) % n_mp if side == 0 else (m + n_mp - 1) % n_mp
        at = pl.ds(h * half, half)
        return remote(
            osend.at[d, at], orecv.at[side, d, at], o_snd.at[d, h], o_rcv.at[side, d, h], mp=there
        )

    def project(d):
        lanes = pl.ds(pl.multiple_of(d * cols, cols), cols)
        pout[...] = jnp.dot(sall[...], wo[:, lanes], preferred_element_type=jnp.float32)

    for k in range(n_mp - 1, 0, -1):
        for side, sign in ((0, 1), (1, -1)):
            d = m + sign * k
            inside = (d <= n_mp - 1) if side == 0 else (d >= 0)
            first = (m == 0) if side == 0 else (m == n_mp - 1)

            @pl.when(inside)
            def _():
                project(d)
                for h in range(HALVES):
                    at = pl.ds(h * half, half)

                    @pl.when(first)
                    def _():
                        osend[d, at, :] = pout[at, :].astype(jnp.bfloat16)

                    @pl.when(jnp.logical_not(first))
                    def _():
                        hop(side, d, h).wait_recv()
                        osend[d, at, :] = (pout[at, :] + orecv[side, d, at, :].astype(jnp.float32)).astype(
                            jnp.bfloat16
                        )

                    hop(side, d, h).start()

    project(m)
    for side in range(2):

        @pl.when(m > 0 if side == 0 else m < n_mp - 1)
        def _():
            for h in range(HALVES):
                at = pl.ds(h * half, half)
                hop(side, m, h).wait_recv()
                pout[at, :] = pout[at, :] + orecv[side, m, at, :].astype(jnp.float32)

    out_ref[...] = pout[...].astype(jnp.bfloat16)

    for p in range(PIECES):
        for k in range(n_mp):
            for side, sign in ((0, -1), (1, 1)):
                b = m + sign * k

                @pl.when(not_last(side) & (b >= 0) & (b <= n_mp - 1))
                def _():
                    z_copy(side, tok_ref.at[piece(p)], b, p, k).wait_send()

            plane_copy(tok_ref.at[piece(p)], k, p).wait_send()

    for copy in sq_copies + f_copies + forward + partial + spread:
        copy.wait_send()
    for d in range(n_mp):

        @pl.when(d != m)
        def _():
            for h in range(HALVES):
                hop(0, d, h).wait_send()


def fused(n_seq, n_mp, tokens, norm_gain, w_cand, w_gate, rec_gate, rec_cand, bias_gate, w_out):
    rows, width = tokens.shape
    k_own, channels = w_cand.shape
    n_chip = n_seq // CORES
    length = rows * n_seq
    bf16, f32 = (jnp.bfloat16, jnp.float32)
    vmem, dma = (pltpu.VMEM, pltpu.SemaphoreType.DMA)
    whole = pl.BlockSpec(memory_space=pltpu.VMEM)
    far = pl.BlockSpec(memory_space=pl.ANY)
    per_channel = [part.reshape(n_seq, LANES) for part in (rec_gate, rec_cand, bias_gate)]
    return pl.pallas_call(
        functools.partial(fused_kernel, n_seq, n_mp),
        out_shape=jax.ShapeDtypeStruct((rows, width), bf16),
        in_specs=[whole, whole, far, far, whole, whole, whole, far],
        out_specs=whole,
        scratch_shapes=[
            vmem((n_mp, rows, width), bf16),
            vmem((length, width), bf16),
            vmem((length // PIECES, width), bf16),
            vmem((n_seq, LANES), f32),
            vmem((n_mp, n_seq, LANES), f32),
            vmem((n_seq, LANES), f32),
            vmem((n_seq, n_seq, LANES), f32),
            vmem((length, LANES), f32),
            vmem((n_chip, k_own * CORES, 2 * LANES), bf16),
            vmem(w_out.shape, bf16),
            vmem((length, 2 * LANES), f32),
            vmem((n_chip - 1, length, 2 * LANES), bf16),
            vmem((n_chip - 1, length, 2 * LANES), bf16),
            vmem((length, LANES), f32),
            vmem((length, LANES), f32),
            vmem((rows, n_seq, LANES), f32),
            vmem((rows, n_seq, LANES), f32),
            vmem((n_seq, LANES), f32),
            vmem((n_seq, rows, LANES), bf16),
            vmem((rows, channels), bf16),
            vmem((rows, width), f32),
            vmem((n_mp, rows, width), bf16),
            vmem((2, n_mp, rows, width), bf16),
            dma((2, n_chip)),
            dma((2, n_chip)),
            dma((2, n_chip)),
            dma,
            dma((2, n_mp, PIECES)),
            dma((n_mp, PIECES)),
            dma((n_mp, PIECES)),
            dma((PIECES, n_seq)),
            dma((n_chip, PIECES)),
            dma((n_mp,)),
            dma((n_mp,)),
            dma((n_seq,)),
            dma((n_seq,)),
            dma((n_chip, PIECES)),
            dma((n_chip, PIECES)),
            dma((n_seq,)),
            dma((n_seq,)),
            dma((n_mp, HALVES)),
            dma((2, n_mp, HALVES)),
        ],
        compiler_params=pltpu.CompilerParams(collective_id=0, has_side_effects=True),
    )(tokens, norm_gain.reshape(n_mp, -1), w_cand, w_gate, *per_channel, w_out)


def layer(n_seq, n_mp, *args):
    tokens, w_cand = (args[0], args[2])
    fits = (
        n_seq == SUBLANES
        and n_seq // CORES == n_mp
        and w_cand.shape[1] == n_seq * LANES
        and tokens.shape[0] == LANES
        and tokens.shape[1] % LANES == 0
    )
    return fused(n_seq, n_mp, *args) if fits else per_device(*args)


def solution(mesh):
    placed = (
        P("seq", "mp"),
        P(),
        P("seq", "mp"),
        P("seq", "mp"),
        P("mp"),
        P("mp"),
        P("mp"),
        P("mp", None),
    )
    return jax.shard_map(
        functools.partial(layer, mesh.shape["seq"], mesh.shape["mp"]), mesh=mesh, in_specs=placed, out_specs=P("seq", "mp"), check_vma=False
    )
```

time: 102 us -> 88.5 us (0.87)
  Pallas kernels: 99.8 us -> 85.2 us
  local copies, waits for them, and re-layouts: 1.67 us -> 3 us
    pallas_call x1, Pallas kernels: 99.8 us -> 85.2 us  [fused(): pl.pallas_call(functools.partial(fused_kernel, n_seq, n_mp), out_shape=ja...]
    reshape x0 -> x1, local copies, waits for them, and re-layouts: none -> 1.33 us  [fused(): norm_gain.reshape(n_mp, -1)]
where the time goes in v2:
time: 88.5 us; the launch traced here: 88.2 us
  Pallas kernels  85.2 us (96%)
  local copies, waits for them, and re-layouts  3 us (3%)
    pallas_call x1, Pallas kernels, fused(): pl.pallas_call(functools.partial(fused_kernel, n_seq, n_mp), out_shape=ja...  85.2 us

profile of v2, /device:TPU:0, one launch (start us, length us, event | category | flops | bytes accessed | tf_op | source)
XLA Modules:
  0.0 88.2 jit_solution(16993925911962060882)
XLA Ops:
  0.0 1.3 %reshape.12.gain_ref = f32[4,1024]{1,0:T(4,128)} reshape(f32[4096]{0:T(1024)} %param.9) | data formatting | bytes 32768 | tf_op jit(solution)/shard_map/reshape | solution.py:548
  1.3 85.2 %shard_map.82 = bf16[128,1024]{1,0:T(8,128)(2,1)} custom-call(bf16[128,1024]{1,0:T(8,128)(2,1)} %tok_ref.1, f32[4,1024]{1,0:T(4,128)} %reshape.12.gain_ref, bf16[512,1024]{1,0:T(8,128)(2,1)} %wc_hbm.1, bf16[512,1024]{1,0:T(8,128)(2,1)} %wg_hbm.1, f32[8,128]{1,0:T(8,128)} %bitcast.3, f32[8,128]{1,0:T(8,128)} %bitcast.4, f32[8,128]{1,0:T(8,128)} %bitcast.5, ...), custom_call_target="tpu_custom_call" | custom-call | tf_op jit(solution)/shard_map/pallas_call | solution.py:498
  86.6 1.7 %copy.10 = bf16[128,1024]{1,0:T(8,128)(2,1)} copy(bf16[128,1024]{1,0:T(8,128)(2,1)} %shard_map.82) | data formatting | bytes 524288

commit v3 on v2

--- a/solution.py
+++ b/solution.py
@@ -106,6 +106,7 @@
     wk,
     wo,
     own,
+    onward,
     psend,
     precv,
     cand_n,
@@ -258,13 +259,15 @@
     rec_gate = rg_ref[pl.ds(q, 1), :]
     rec_cand = rc_ref[pl.ds(q, 1), :]
     tile = n_seq * part
-    forward, partial, f_copies = ([], [], [])
-
-    def stage_a(p):
+    forward, f_copies = ([], [])
+
+    def stage_a(turn):
+        if turn + 2 < PIECES:
+            send_own(turn + 2)
         for k in range(1, n_mp):
-            pass_on(p, k)
-            if k == 1 and p + 2 < PIECES:
-                send_own(p + 2)
+            p = turn - (k - 1)
+            if 0 <= p < PIECES:
+                pass_on(p, k)
 
     def factors():
         total = sq_own[...]
@@ -315,50 +318,66 @@
             of = pl.ds(pl.multiple_of(p * tile + i * GROUP, GROUP), GROUP)
             xn[at, :] = (xk[of, :].astype(jnp.float32) * f_col[of, 0:1] * gain).astype(jnp.bfloat16)
 
+        def product(chip):
+            return jnp.dot(xn[...], wk[chip], preferred_element_type=jnp.float32)
+
         at = pl.ds(p * tile, tile)
-        for o in list(range(1, n_chip)) + [0]:
-            chip = (c + o) % n_chip
-            value = jnp.dot(xn[...], wk[chip], preferred_element_type=jnp.float32)
-            if o == 0:
-                own[at, :] = value
-            else:
-                psend[o - 1, at, :] = value.astype(jnp.bfloat16)
-                copy = remote(
-                    psend.at[o - 1, at],
-                    precv.at[o - 1, at],
-                    p_snd.at[o, p],
-                    p_rcv.at[o, p],
-                    seq=chip * CORES + r,
-                )
-                copy.start()
-                partial.append(copy)
-
-    for turn in range(PIECES + 2):
-        if turn < PIECES:
-            stage_a(turn)
+        first, second = ends(p)
+        psend[1, at, :] = product(n_chip - 1 - c).astype(jnp.bfloat16)
+        sums(1, p, first).start()
+        psend[0, at, :] = product(first).astype(jnp.bfloat16)
+        sums(0, p, first).start()
+        onward[at, :] = product(second)
+        own[at, :] = product(c)
+
+    def ends(p):
+        beside, above = (c + 1 - 2 * (c % 2), (c + n_chip // 2) % n_chip)
+        return (beside, above) if p % 2 == 0 else (above, beside)
+
+    def sums(slot, p, chip):
+        at = pl.ds(p * tile, tile)
+        return remote(
+            psend.at[slot, at], precv.at[slot, at], p_snd.at[slot, p], p_rcv.at[slot, p], seq=chip * CORES + r
+        )
+
+    def stage_d(p):
+        _, second = ends(p)
+        sums(1, p, second).wait_recv()
+
+        @pl.loop(0, tile // GROUP)
+        def _(i):
+            at = pl.ds(pl.multiple_of(p * tile + i * GROUP, GROUP), GROUP)
+            psend[2, at, :] = (onward[at, :] + precv[1, at, :].astype(jnp.float32)).astype(jnp.bfloat16)
+
+        sums(2, p, second).start()
+
+    for turn in range(PIECES + n_mp + 1):
+        stage_a(turn)
         if turn == 0:
             factors()
-        if 0 <= turn - 1 < PIECES:
-            stage_b(turn - 1)
         if turn == 1:
             spread_factors()
             for copy in local:
                 copy.wait()
             for copy in w_out_copies:
                 copy.wait()
-        if 0 <= turn - 2 < PIECES:
-            stage_c(turn - 2)
+        if 0 <= turn - n_mp < PIECES:
+            stage_c(turn - n_mp)
+        if 0 <= turn - (n_mp + 1) < PIECES:
+            stage_d(turn - (n_mp + 1))
+        if 0 <= turn - (n_mp - 1) < PIECES:
+            stage_b(turn - (n_mp - 1))
 
     def gather_piece(p):
-        for copy in partial[p * (n_chip - 1) : (p + 1) * (n_chip - 1)]:
-            copy.wait_recv()
+        for slot in (0, 2):
+            sums(slot, p, c).wait_recv()
 
         @pl.loop(0, tile // GROUP)
         def _(i):
             at = pl.ds(pl.multiple_of(p * tile + i * GROUP, GROUP), GROUP)
             value = own[at, :]
-            for o in range(n_chip - 1):
-                value = value + precv[o, at, :].astype(jnp.float32)
+            for slot in (0, 2):
+                value = value + precv[slot, at, :].astype(jnp.float32)
             cand_n[at, :] = value[:, :LANES]
             gate_n[at, :] = value[:, LANES:] + bias
 
@@ -474,8 +493,10 @@
                     z_copy(side, tok_ref.at[piece(p)], b, p, k).wait_send()
 
             plane_copy(tok_ref.at[piece(p)], k, p).wait_send()
-
-    for copy in sq_copies + f_copies + forward + partial + spread:
+        for slot in range(3):
+            sums(slot, p, c).wait_send()
+
+    for copy in sq_copies + f_copies + forward + spread:
         copy.wait_send()
     for d in range(n_mp):
 
@@ -511,6 +532,7 @@
             vmem((length, LANES), f32),
             vmem((n_chip, k_own * CORES, 2 * LANES), bf16),
             vmem(w_out.shape, bf16),
+            vmem((length, 2 * LANES), f32),
             vmem((length, 2 * LANES), f32),
             vmem((n_chip - 1, length, 2 * LANES), bf16),
             vmem((n_chip - 1, length, 2 * LANES), bf16),
@@ -552,6 +574,7 @@
     tokens, w_cand = (args[0], args[2])
     fits = (
         n_seq == SUBLANES
+        and n_seq == 4 * CORES
         and n_seq // CORES == n_mp
         and w_cand.shape[1] == n_seq * LANES
         and tokens.shape[0] == LANES

time: 88.5 us -> 86.6 us (0.979)
  Pallas kernels: 85.2 us -> 83.4 us
    pallas_call x1, Pallas kernels: 85.2 us -> 83.4 us  [fused(): pl.pallas_call(functools.partial(fused_kernel, n_seq, n_mp), out_shape=ja...]
where the time goes in v3:
time: 86.6 us; the launch traced here: 86.4 us
  Pallas kernels  83.4 us (96%)
  local copies, waits for them, and re-layouts  3 us (3%)
    pallas_call x1, Pallas kernels, fused(): pl.pallas_call(functools.partial(fused_kernel, n_seq, n_mp), out_shape=ja...  83.4 us

profile of v3, /device:TPU:0, one launch (start us, length us, event | category | flops | bytes accessed | tf_op | source)
XLA Modules:
  0.0 86.4 jit_solution(5568530948321829318)
XLA Ops:
  0.0 1.3 %reshape.12.gain_ref = f32[4,1024]{1,0:T(4,128)} reshape(f32[4096]{0:T(1024)} %param.9) | data formatting | bytes 32768 | tf_op jit(solution)/shard_map/reshape | solution.py:570
  1.3 83.4 %shard_map.82 = bf16[128,1024]{1,0:T(8,128)(2,1)} custom-call(bf16[128,1024]{1,0:T(8,128)(2,1)} %tok_ref.1, f32[4,1024]{1,0:T(4,128)} %reshape.12.gain_ref, bf16[512,1024]{1,0:T(8,128)(2,1)} %wc_hbm.1, bf16[512,1024]{1,0:T(8,128)(2,1)} %wg_hbm.1, f32[8,128]{1,0:T(8,128)} %bitcast.3, f32[8,128]{1,0:T(8,128)} %bitcast.4, f32[8,128]{1,0:T(8,128)} %bitcast.5, ...), custom_call_target="tpu_custom_call" | custom-call | tf_op jit(solution)/shard_map/pallas_call | solution.py:519
  84.7 1.7 %copy.10 = bf16[128,1024]{1,0:T(8,128)(2,1)} copy(bf16[128,1024]{1,0:T(8,128)(2,1)} %shard_map.82) | data formatting | bytes 524288

commit v4 on v3

--- a/solution.py
+++ b/solution.py
@@ -77,7 +77,7 @@
 CORES = 2
 SUBLANES = 8
 LANES = 128
-PIECES = 4
+PIECES = 8
 HALVES = 2
 GROUP = 16
 MESH = pl.DeviceIdType.MESH
@@ -363,10 +363,10 @@
                 copy.wait()
         if 0 <= turn - n_mp < PIECES:
             stage_c(turn - n_mp)
+        if 0 <= turn - (n_mp - 1) < PIECES:
+            stage_b(turn - (n_mp - 1))
         if 0 <= turn - (n_mp + 1) < PIECES:
             stage_d(turn - (n_mp + 1))
-        if 0 <= turn - (n_mp - 1) < PIECES:
-            stage_b(turn - (n_mp - 1))
 
     def gather_piece(p):
         for slot in (0, 2):

time: 86.6 us -> 85.7 us (0.990)
  Pallas kernels: 83.4 us -> 82.5 us
    pallas_call x1, Pallas kernels: 83.4 us -> 82.5 us  [fused(): pl.pallas_call(functools.partial(fused_kernel, n_seq, n_mp), out_shape=ja...]
where the time goes in v4:
time: 85.7 us; the launch traced here: 85.5 us
  Pallas kernels  82.5 us (96%)
  local copies, waits for them, and re-layouts  3 us (4%)
    pallas_call x1, Pallas kernels, fused(): pl.pallas_call(functools.partial(fused_kernel, n_seq, n_mp), out_shape=ja...  82.5 us

profile of v4, /device:TPU:0, one launch (start us, length us, event | category | flops | bytes accessed | tf_op | source)
XLA Modules:
  0.0 85.5 jit_solution(6455330265855773272)
XLA Ops:
  0.0 1.3 %reshape.12.gain_ref = f32[4,1024]{1,0:T(4,128)} reshape(f32[4096]{0:T(1024)} %param.9) | data formatting | bytes 32768 | tf_op jit(solution)/shard_map/reshape | solution.py:570
  1.3 82.5 %shard_map.82 = bf16[128,1024]{1,0:T(8,128)(2,1)} custom-call(bf16[128,1024]{1,0:T(8,128)(2,1)} %tok_ref.1, f32[4,1024]{1,0:T(4,128)} %reshape.12.gain_ref, bf16[512,1024]{1,0:T(8,128)(2,1)} %wc_hbm.1, bf16[512,1024]{1,0:T(8,128)(2,1)} %wg_hbm.1, f32[8,128]{1,0:T(8,128)} %bitcast.3, f32[8,128]{1,0:T(8,128)} %bitcast.4, f32[8,128]{1,0:T(8,128)} %bitcast.5, ...), custom_call_target="tpu_custom_call" | custom-call | tf_op jit(solution)/shard_map/pallas_call | solution.py:519
  83.8 1.7 %copy.10 = bf16[128,1024]{1,0:T(8,128)(2,1)} copy(bf16[128,1024]{1,0:T(8,128)(2,1)} %shard_map.82) | data formatting | bytes 524288
